TPU v7x, 32 devices: a whole 2x2x4 slice. The times are simulated.
32 devices in a mesh: dp: 8 (over z, y), tp: 4 (over x, core).
Axes of the slice: x: 2, y: 2, z: 4, core: 2. Of those that a mesh axis runs over, the one named last changes fastest.
Arguments:
- inputs: bfloat16 [16384, 2048], P(('dp', 'tp')), may hold values from -6 to 6
- sentence_ids: int32 [32, 512], P(('dp', 'tp')), may hold values from 0 to 3, never falling along the last dimension, each value on 1 to 192 neighbouring positions
- start_states: float32 [128, 2048], P(('dp', 'tp')), may hold values from -5 to 5
- ln_gain: float32 [2048], replicated, may hold values from 0.1 to 1.9
- ln_bias: float32 [2048], replicated, may hold values from -3 to 3
- weight: bfloat16 [6144, 2048], P('tp'), may hold values from -0.125 to 0.125
- gate_bias: float32 [2, 2048], replicated, may hold values from -2 to 4
- out_grad: bfloat16 [16384, 2048], P(('dp', 'tp')), may hold values from -6 to 6
Outputs:
- output: bfloat16 [16384, 2048], P(('dp', 'tp'))
- final_states: float32 [128, 2048], P(('dp', 'tp'))
- input_grad: float32 [16384, 2048], P(('dp', 'tp'))
- weight_grad: float32 [6144, 2048], P('tp')
- gate_bias_grad: float32 [2, 2048], replicated
- ln_gain_grad: float32 [2048], replicated
- ln_bias_grad: float32 [2048], replicated
- start_grad: float32 [128, 2048], P(('dp', 'tp'))
Inputs may be any that keep to these rules, and one draw needn't show every extreme that they name: `sentence_ids`: each row holds the sentence ids of one device's tokens in order: never falling, every id of 0 to 3 present, each sentence 1 to 192 tokens and some sentence exactly 192.
All inputs are finite; a program needn't handle non-finite values.
Results may differ from a plain program's by a relative error of at most 0.006.
Values may be sent and summed in bfloat16 or wider, within the bound.
No kernel may reach another device: no remote copies, remote signals or barrier semaphores. Data moves between devices by JAX's collectives and lax.ppermute only.
A program may use at most 256 MiB of HBM per device.

v0:
```python
import jax
import jax.numpy as jnp
from jax import lax
from jax.sharding import PartitionSpec as P

SENT_DEV = 4


def link(first, second):
    first_decay, first_value = first
    second_decay, second_value = second
    return (first_decay * second_decay, second_decay * first_value + second_value)


def local(inputs, sentence_ids, start_states, ln_gain, ln_bias, weight, gate_bias, out_grad):
    width = inputs.shape[1]
    signal = inputs.astype(jnp.float32)
    centred = signal - jnp.mean(signal, axis=1, keepdims=True)
    rstd = lax.rsqrt(jnp.mean(centred * centred, axis=1, keepdims=True) + 1e-05)
    scaled_in = centred * rstd
    normed = scaled_in * ln_gain + ln_bias
    normed_low = normed.astype(jnp.bfloat16)
    contract_last = (((1,), (1,)), ((), ()))
    contract_first = (((0,), (0,)), ((), ()))
    streams = lax.dot_general(
        normed_low,
        lax.all_gather(weight, "tp", axis=0, tiled=True),
        contract_last,
        preferred_element_type=jnp.float32,
    ).astype(jnp.bfloat16)
    stream_vals = streams.astype(jnp.float32)
    candidate = stream_vals[:, :width]
    forget = jax.nn.sigmoid(stream_vals[:, width : 2 * width] + gate_bias[0])
    reset = jax.nn.sigmoid(stream_vals[:, 2 * width :] + gate_bias[1])
    seg_row = sentence_ids[0]
    first_mask = jnp.concatenate([jnp.ones((1,), bool), seg_row[1:] != seg_row[:-1]])[:, None]
    last_mask = jnp.concatenate([seg_row[:-1] != seg_row[1:], jnp.ones((1,), bool)])[:, None]
    table = (seg_row[:, None] == jnp.arange(SENT_DEV, dtype=jnp.int32)[None, :]).astype(jnp.float32)
    begin = jnp.dot(table, start_states, precision=lax.Precision.HIGHEST)
    zeros_like = jnp.zeros_like(forget)
    decay = jnp.where(first_mask, zeros_like, forget)
    drive = (1.0 - forget) * candidate + jnp.where(first_mask, forget * begin, zeros_like)
    unused, cells = lax.associative_scan(link, (decay, drive), axis=0)
    output = (signal + reset * cells + (1.0 - reset) * normed).astype(jnp.bfloat16)
    picker = table * last_mask.astype(jnp.float32)
    final_states = lax.dot_general(picker, cells, contract_first, precision=lax.Precision.HIGHEST)
    outer = out_grad.astype(jnp.float32)
    shifted = jnp.concatenate([jnp.zeros((1, width), jnp.float32), cells[:-1]], axis=0)
    previous = jnp.where(first_mask, begin, shifted)
    reset_pre_grad = outer * (cells - normed) * reset * (1.0 - reset)
    direct = outer * reset
    next_decay = jnp.concatenate([decay[1:], jnp.zeros((1, width), jnp.float32)], axis=0)
    unused_back, carry_grad = lax.associative_scan(link, (next_decay, direct), reverse=True, axis=0)
    candidate_grad = carry_grad * (1.0 - forget)
    forget_pre_grad = carry_grad * (previous - candidate) * forget * (1.0 - forget)
    start_terms = jnp.where(first_mask, forget * carry_grad, zeros_like)
    start_grad = lax.dot_general(
        table, start_terms, contract_first, precision=lax.Precision.HIGHEST
    )
    stream_grads = jnp.concatenate(
        [candidate_grad, forget_pre_grad, reset_pre_grad], axis=1
    ).astype(jnp.bfloat16)
    bias_part = jnp.stack([jnp.sum(forget_pre_grad, axis=0), jnp.sum(reset_pre_grad, axis=0)])
    columns = stream_grads
    projected_grad = jnp.dot(
        columns,
        lax.all_gather(weight, "tp", axis=0, tiled=True),
        preferred_element_type=jnp.float32,
    )
    columns = stream_grads
    weight_part = lax.psum_scatter(
        lax.dot_general(columns, normed_low, contract_first, preferred_element_type=jnp.float32),
        "tp",
        scatter_dimension=0,
        tiled=True,
    )
    normed_grad = projected_grad + outer * (1.0 - reset)
    gain_part = jnp.sum(normed_grad * scaled_in, axis=0)
    shift_part = jnp.sum(normed_grad, axis=0)
    scaled_grad = normed_grad * ln_gain
    input_grad = (
        rstd
        * (
            scaled_grad
            - jnp.mean(scaled_grad, axis=1, keepdims=True)
            - scaled_in * jnp.mean(scaled_grad * scaled_in, axis=1, keepdims=True)
        )
        + outer
    )
    weight_grad = lax.psum(weight_part, "dp")
    bias_grad, gain_grad, shift_grad = lax.psum((bias_part, gain_part, shift_part), ("dp", "tp"))
    return (
        output,
        final_states,
        input_grad,
        weight_grad,
        bias_grad,
        gain_grad,
        shift_grad,
        start_grad,
    )


def solution(mesh):
    placed = (
        P(("dp", "tp"), None),
        P(("dp", "tp"), None),
        P(("dp", "tp"), None),
        P(),
        P(),
        P("tp", None),
        P(),
        P(("dp", "tp"), None),
    )
    return jax.shard_map(
        local,
        mesh=mesh,
        in_specs=placed,
        out_specs=(
            P(("dp", "tp"), None),
            P(("dp", "tp"), None),
            P(("dp", "tp"), None),
            P("tp", None),
            P(),
            P(),
            P(),
            P(("dp", "tp"), None),
        ),
        check_vma=False,
    )
```

profile of v0, /device:TPU:0, one launch (start us, length us, event | category | flops | bytes accessed | tf_op | source)
XLA Modules:
  0.0 1565.2 jit_solution(1547898737292328093)
XLA Ops:
  10.5 156.7 %all-gather.2.cloned.1.call-done = bf16[6144,2048]{1,0:T(8,128)(2,1)} async-done(((bf16[1536,2048]{1,0:T(8,128)(2,1)}), bf16[6144,2048]{1,0:T(8,128)(2,1)}) %all-gather.2.cloned.1.call-update) | async-done | bytes 25165840 | tf_op jit(solution)/shard_map/all_gather | solution.py:27
  167.2 19.4 %fusion = f32[512,6144]{1,0:T(8,128)} fusion(bf16[6144,2048]{1,0:T(8,128)(2,1)} %all-gather.2.cloned.1.call-done, bf16[512,2048]{1,0:T(8,128)(2,1)S(1)} %copy-done.4, f32[2048]{0:T(1024)S(1)} %copy-done.30, f32[2048]{0:T(1024)S(1)} %copy-done.20, f32[512]{0:T(512)S(1)} %add_rsqrt_fusion, f32[512]{0:T(512)S(1)} %broadcast_multiply_fusion.2), kind=kOutput, calls=%fused_computation.1 | convolution fusion | flops 12897484800 | bytes 39866368 | tf_op jit(solution)/shard_map/dot_general | solution.py:25
  214.8 10.1 slice.472
  249.4 9.8 slice.540
  260.1 10.0 slice.537
  402.9 16.5 %pad.128 = f32[512,2048]{1,0:T(8,128)} pad(f32[256,2048]{1,0:T(8,128)} %pad_maximum_fusion.3, f32[]{:T(128)} %constant.15.clone.1), padding=0_1_1x0_0_0 | pad | bytes 6291460 | tf_op jit(solution)/shard_map/pad | solution.py:43
  419.3 16.6 %pad.129 = f32[512,2048]{1,0:T(8,128)} pad(f32[256,2048]{1,0:T(8,128)} %add.338, f32[]{:T(128)} %constant.15.clone.1), padding=1_0_1x0_0_0 | pad | bytes 6291460 | tf_op jit(solution)/shard_map/pad | solution.py:43
  463.1 9.9 slice.546
  482.8 16.7 %slice.550 = f32[256,2048]{1,0:T(8,128)} reverse(f32[256,2048]{1,0:T(8,128)} %slice.549), dimensions={0} | reverse | bytes 4194304 | tf_op jit(solution)/shard_map/slice | solution.py:53
  499.4 16.7 %slice.543 = f32[256,2048]{1,0:T(8,128)} reverse(f32[256,2048]{1,0:T(8,128)} %slice.542), dimensions={0} | reverse | bytes 4194304 | tf_op jit(solution)/shard_map/slice | solution.py:53
  516.2 16.6 %slice.545 = f32[256,2048]{1,0:T(8,128)} reverse(f32[256,2048]{1,0:T(8,128)} %slice.544), dimensions={0} | reverse | bytes 4194304 | tf_op jit(solution)/shard_map/slice | solution.py:53
  532.8 16.7 %slice.547 = f32[256,2048]{1,0:T(8,128)} reverse(f32[256,2048]{1,0:T(8,128)} %slice.546), dimensions={0} | reverse | bytes 4194304 | tf_op jit(solution)/shard_map/slice | solution.py:53
  617.8 17.0 %slice.541 = f32[255,2048]{1,0:T(8,128)} reverse(f32[255,2048]{1,0:T(8,128)} %slice.540), dimensions={0} | reverse | bytes 4177920 | tf_op jit(solution)/shard_map/slice | solution.py:53
  634.8 17.1 %slice.611 = f32[255,2048]{1,0:T(8,128)} reverse(f32[255,2048]{1,0:T(8,128)} %slice.610), dimensions={0} | reverse | bytes 4177920 | tf_op jit(solution)/shard_map/slice | solution.py:53
  692.3 16.6 %pad.146 = f32[512,2048]{1,0:T(8,128)} pad(f32[256,2048]{1,0:T(8,128)} %pad_maximum_fusion.4, f32[]{:T(128)} %constant.15.clone.1), padding=0_1_1x0_0_0 | pad | bytes 6291460 | tf_op jit(solution)/shard_map/pad | solution.py:53
  708.9 16.5 %pad.147 = f32[512,2048]{1,0:T(8,128)} pad(f32[256,2048]{1,0:T(8,128)} %add.366, f32[]{:T(128)} %constant.15.clone.1), padding=1_0_1x0_0_0 | pad | bytes 6291460 | tf_op jit(solution)/shard_map/pad | solution.py:53
  732.0 32.6 %rev.2 = f32[512,2048]{1,0:T(8,128)} reverse(f32[512,2048]{1,0:T(8,128)} %add.368), dimensions={0} | reverse | bytes 8388608 | tf_op jit(solution)/shard_map/rev | solution.py:53
  764.7 10.8 fusion.71
  775.5 24.6 %fusion.32 = f32[6144,2048]{1,0:T(8,128)} fusion(bf16[512,2048]{1,0:T(8,128)(2,1)} %get-tuple-element.20, bf16[512,2048]{1,0:T(8,128)(2,1)} %get-tuple-element.18, bf16[512,2048]{1,0:T(8,128)(2,1)} %get-tuple-element.22, bf16[512,2048]{1,0:T(8,128)(2,1)S(1)} %copy-done.4, f32[2048]{0:T(1024)S(1)} %copy-done.32, f32[2048]{0:T(1024)S(1)} %copy-done.20, ...), kind=kOutput, calls=%fused_computation.48 | convolution fusion | flops 12910067712 | bytes 58740736 | tf_op jit(solution)/shard_map/dot_general | solution.py:72
  800.2 346.6 %reduce-scatter.2.cloned.1.call-done = f32[1536,2048]{1,0:T(8,128)} async-done(((f32[6144,2048]{1,0:T(8,128)}), f32[1536,2048]{1,0:T(8,128)}) %reduce-scatter.2.cloned.1.call-update) | async-done | bytes 12582928 | tf_op jit(solution)/shard_map/reduce_scatter | solution.py:71
  1147.6 27.8 %fusion.16 = (f32[2048]{0:T(1024)S(1)}, f32[512]{0:T(512)S(1)}, f32[512]{0:T(512)S(1)}, f32[2048]{0:T(1024)S(1)}, f32[512,2048]{1,0:T(8,128)}) fusion(bf16[512,2048]{1,0:T(8,128)(2,1)S(1)} %copy-done.4, f32[512]{0:T(512)S(1)} %copy-done.28, f32[512]{0:T(512)S(1)} %copy-done.23, f32[2048]{0:T(1024)S(1)} %copy-done.20, f32[2048]{0:T(1024)S(1)} %bitcast.12, ...), kind=kOutput, calls=%fused_computation.25 | convolution fusion | flops 12922646528 | bytes 44081152 | tf_op jit(solution)/shard_map/dot_general | solution.py:65
  1175.4 43.3 %all-reduce.38 = (f32[2,2048]{1,0:T(2,128)}, f32[2048]{0:T(1024)}, f32[2048]{0:T(1024)}) all-reduce(f32[2,2048]{1,0:T(2,128)S(1)} %pad_maximum_fusion.19, f32[2048]{0:T(1024)S(1)} %get-tuple-element.8, f32[2048]{0:T(1024)S(1)} %get-tuple-element.11), channel_id=1, replica_groups=mesh['dp'=8,'tp'=4] {'dp','tp'}, use_global_device_ids=true, to_apply=%region_8.9 | all-reduce | flops 8192 | bytes 65536 | tf_op jit(solution)/shard_map/psum | solution.py:91
  1233.7 313.0 %all-reduce.41.cloned.1.call-done = f32[1536,2048]{1,0:T(8,128)} async-done(((f32[1536,2048]{1,0:T(8,128)}), f32[1536,2048]{1,0:T(8,128)}) %all-reduce.41.cloned.1.call-update) | async-done | bytes 12582928 | tf_op jit(solution)/shard_map/psum | solution.py:90
  1546.7 11.5 copy.17
  (293 shorter events, 356.8 us)
Async XLA Ops:
  7.2 179.4 %copy-start = (f32[4,2048]{1,0:T(4,128)S(1)}, f32[4,2048]{1,0:T(4,128)}, u32[]{:S(2)}) copy-start(f32[4,2048]{1,0:T(4,128)} %param.10) | copy-start | bytes 98308
  7.2 159.9 %copy-start.20 = (f32[2048]{0:T(1024)S(1)}, f32[2048]{0:T(1024)}, u32[]{:S(2)}) copy-start(f32[2048]{0:T(1024)} %param.11) | copy-start | bytes 24580
  7.2 159.9 %copy-start.30 = (f32[2048]{0:T(1024)S(1)}, f32[2048]{0:T(1024)}, u32[]{:S(2)}) copy-start(f32[2048]{0:T(1024)} %param.12) | copy-start | bytes 24580
  7.2 159.9 %all-gather.2.cloned.1.call-start = ((), (), s32[]{:S(2)}) async-start(), calls=%async_computation.1 | async-start | bytes 31457280 | tf_op jit(solution)/shard_map/all_gather | solution.py:27
  8.0 1138.8 %reduce-scatter.2.cloned.1.call-start = ((), (), s32[]{:S(2)}) async-start(), calls=%async_computation.2 | async-start | bytes 62914560 | tf_op jit(solution)/shard_map/reduce_scatter | solution.py:71
  8.8 177.8 %copy-start.34 = (pred[512]{0:T(512)(128)(4,1)}, pred[512]{0:T(512)(128)(4,1)S(1)}, u32[]{:S(2)}) copy-start(pred[512]{0:T(512)(128)(4,1)S(1)} %pad_add_fusion.2) | copy-start | bytes 1540
  9.2 177.4 %copy-start.22 = (f32[512]{0:T(512)}, f32[512]{0:T(512)S(1)}, u32[]{:S(2)}) copy-start(f32[512]{0:T(512)S(1)} %broadcast_multiply_fusion.2) | copy-start | bytes 6148
  9.9 176.7 %copy-start.26 = (f32[512]{0:T(512)}, f32[512]{0:T(512)S(1)}, u32[]{:S(2)}) copy-start(f32[512]{0:T(512)S(1)} %add_rsqrt_fusion) | copy-start | bytes 6148
  355.5 7.0 copy-start.19
  379.4 9.8 copy-start.15
  436.0 6.9 copy-start.2
  436.0 6.9 copy-start.3
  436.0 8.0 copy-start.13
  436.0 8.0 copy-start.21
  436.0 8.0 copy-start.23
  436.0 8.0 copy-start.27
  436.0 8.0 copy-start.31
  634.8 17.5 %copy-start.18 = (f32[15,2048]{1,0:T(8,128)S(1)}, f32[15,2048]{1,0:T(8,128)}, u32[]{:S(2)}) copy-start(f32[15,2048]{1,0:T(8,128)} %slice.569) | copy-start | bytes 368644
  668.8 9.8 copy-start.16
  732.0 32.6 %copy-start.35 = (pred[512]{0:T(512)(128)(4,1)S(1)}, pred[512]{0:T(512)(128)(4,1)}, u32[]{:S(2)}) copy-start(pred[512]{0:T(512)(128)(4,1)} %copy-done.34) | copy-start | bytes 1540
  764.7 10.8 copy-start.32
  800.1 746.5 %all-reduce.41.cloned.1.call-start = ((), (), s32[]{:S(2)}) async-start(), calls=%async_computation.3 | async-start | bytes 25165824 | tf_op jit(solution)/shard_map/psum | solution.py:90
  1147.6 71.2 %copy-start.25 = (s32[1,512]{1,0:T(1,128)S(1)}, s32[1,512]{1,0:T(1,128)}, u32[]{:S(2)}) copy-start(s32[1,512]{1,0:T(1,128)} %param.9) | copy-start | bytes 6148
  1546.7 11.6 copy-start.1
  (15 other events, 50.9 us)
Sparse Core Ops, SparseCore 0:
  9.6 157.4 all-gather.1
  800.3 346.4 reduce-scatter.1
  1150.9 395.7 all-reduce.40
where the time goes:
time: 1590 us; the launch traced here: 1570 us
  waiting for transfers between devices  817 us (51%)
  local copies, waits for them, and re-layouts  495 us (31%)
  other arithmetic  102 us (6%)
  matrix products  92.1 us (6%)
  blocking collectives  43.3 us (3%)
    reduce_scatter x1, waiting for transfers between devices, local(): lax.psum_scatter(lax.dot_general(columns, normed_low, contract_first, pre...  347 us
    psum x1, waiting for transfers between devices, local(): weight_grad = lax.psum(weight_part, 'dp')  313 us
    slice x59, local copies, waits for them, and re-layouts, local(): lax.associative_scan(link, (next_decay, direct), reverse=True, axis=0)  214 us
    all_gather x1, waiting for transfers between devices, local(): lax.all_gather(weight, 'tp', axis=0, tiled=True)  157 us
    slice x53, local copies, waits for them, and re-layouts, local(): unused, cells = lax.associative_scan(link, (decay, drive), axis=0)  117 us
    pad x16, local copies, waits for them, and re-layouts, local(): lax.associative_scan(link, (next_decay, direct), reverse=True, axis=0)  54.8 us
    pad x16, local copies, waits for them, and re-layouts, local(): unused, cells = lax.associative_scan(link, (decay, drive), axis=0)  54.5 us
    psum x1, blocking collectives, local(): lax.psum((bias_part, gain_part, shift_part), ('dp', 'tp'))  43.3 us
  transfers between devices with their start and end apart: 3, of which 3 were waited for; matrix products, arithmetic and copies ran while one was open for 3% of the time, Pallas kernels for 0%

commit v1 on v0

--- a/solution.py
+++ b/solution.py
@@ -87,7 +87,12 @@
         )
         + outer
     )
-    weight_grad = lax.psum(weight_part, "dp")
+
+    def guide_lanes(frame_in):
+        a_now = lax.all_gather(frame_in, axis_name="dp")
+        return jnp.sum(a_now, axis=0)
+
+    weight_grad = guide_lanes(weight_part)
     bias_grad, gain_grad, shift_grad = lax.psum((bias_part, gain_part, shift_part), ("dp", "tp"))
     return (
         output,

time: 1590 us -> 3110 us (1.96)
  waiting for transfers between devices: 817 us -> 2210 us
  blocking collectives: 43.3 us -> 153 us
  other arithmetic: 102 us -> 138 us
    all_gather x0 -> x1, waiting for transfers between devices: none -> 1700 us  [guide_lanes(): a_now = lax.all_gather(frame_in, axis_name='dp')]
    psum x1 -> x0, waiting for transfers between devices: 313 us -> none  [local(): weight_grad = lax.psum(weight_part, 'dp')]
    psum x1, blocking collectives: 43.3 us -> 153 us  [local(): lax.psum((bias_part, gain_part, shift_part), ('dp', 'tp'))]
    reduce_sum x0 -> x1, other arithmetic: none -> 36.2 us  [guide_lanes(): return jnp.sum(a_now, axis=0)]
  transfers between devices with their start and end apart: 3 -> 3, of which waited for: 3 -> 3; matrix products, arithmetic and copies ran while one was open for 3% -> 1% of each run, Pallas kernels for 0% -> 0%
where the time goes in v1:
time: 3110 us; the launch traced here: 3090 us
  waiting for transfers between devices  2210 us (71%)
  local copies, waits for them, and re-layouts  483 us (16%)
  blocking collectives  153 us (5%)
  other arithmetic  138 us (4%)
  matrix products  92.4 us (3%)
    all_gather x1, waiting for transfers between devices, guide_lanes(): a_now = lax.all_gather(frame_in, axis_name='dp')  1700 us
    reduce_scatter x1, waiting for transfers between devices, local(): lax.psum_scatter(lax.dot_general(columns, normed_low, contract_first, pre...  347 us
    slice x59, local copies, waits for them, and re-layouts, local(): lax.associative_scan(link, (next_decay, direct), reverse=True, axis=0)  214 us
    all_gather x1, waiting for transfers between devices, local(): lax.all_gather(weight, 'tp', axis=0, tiled=True)  157 us
    psum x1, blocking collectives, local(): lax.psum((bias_part, gain_part, shift_part), ('dp', 'tp'))  153 us
    slice x53, local copies, waits for them, and re-layouts, local(): unused, cells = lax.associative_scan(link, (decay, drive), axis=0)  117 us
  transfers between devices with their start and end apart: 3, of which 3 were waited for; matrix products, arithmetic and copies ran while one was open for 1% of the time, Pallas kernels for 0%

profile of v1, /device:TPU:0, one launch (start us, length us, event | category | flops | bytes accessed | tf_op | source)
XLA Modules:
  0.0 3088.7 jit_solution(3788173662014707168)
XLA Ops:
  10.5 156.7 %all-gather.4.cloned.1.call-done = bf16[6144,2048]{1,0:T(8,128)(2,1)} async-done(((bf16[1536,2048]{1,0:T(8,128)(2,1)}), bf16[6144,2048]{1,0:T(8,128)(2,1)}) %all-gather.4.cloned.1.call-update) | async-done | bytes 25165840 | tf_op jit(solution)/shard_map/all_gather | solution.py:27
  167.2 19.4 fusion
  214.8 10.1 slice.472
  260.1 10.0 slice.537
  403.0 16.5 pad.128
  419.4 16.7 pad.129
  453.3 9.8 slice.610
  473.0 9.9 slice.544
  482.8 16.7 slice.550
  499.6 16.7 slice.543
  516.3 16.6 slice.545
  532.9 16.7 slice.547
  617.9 17.0 slice.541
  634.9 17.1 slice.611
  692.3 16.5 pad.146
  708.8 16.5 pad.147
  731.8 32.6 %rev.2 = f32[512,2048]{1,0:T(8,128)} reverse(f32[512,2048]{1,0:T(8,128)} %add.366), dimensions={0} | reverse | bytes 8388608 | tf_op jit(solution)/shard_map/rev | solution.py:53
  764.4 10.8 fusion.71
  775.2 24.6 fusion.32
  799.9 346.6 %reduce-scatter.2.cloned.1.call-done = f32[1536,2048]{1,0:T(8,128)} async-done(((f32[6144,2048]{1,0:T(8,128)}), f32[1536,2048]{1,0:T(8,128)}) %reduce-scatter.2.cloned.1.call-update) | async-done | bytes 12582928 | tf_op jit(solution)/shard_map/reduce_scatter | solution.py:71
  1147.2 27.9 fusion.16
  1175.1 152.7 %all-reduce.38 = (f32[2,2048]{1,0:T(2,128)}, f32[2048]{0:T(1024)}, f32[2048]{0:T(1024)}) all-reduce(f32[2,2048]{1,0:T(2,128)S(1)} %pad_maximum_fusion.19, f32[2048]{0:T(1024)S(1)} %get-tuple-element.8, f32[2048]{0:T(1024)S(1)} %get-tuple-element.11), channel_id=1, replica_groups=mesh['dp'=8,'tp'=4] {'dp','tp'}, use_global_device_ids=true, to_apply=%region_8.9 | all-reduce | flops 8192 | bytes 65536 | tf_op jit(solution)/shard_map/psum | solution.py:96
  1342.8 1702.7 %all-gather.6.cloned.1.call-done = f32[12288,2048]{1,0:T(8,128)} async-done(((f32[1536,2048]{1,0:T(8,128)}), f32[12288,2048]{1,0:T(8,128)}) %all-gather.6.cloned.1.call-update) | async-done | bytes 100663312 | tf_op jit(solution)/shard_map/all_gather | solution.py:92
  3045.5 36.2 %reduce_sum.85 = f32[1536,2048]{1,0:T(8,128)} reduce(f32[8,1536,2048]{2,1,0:T(8,128)} %bitcast.3, f32[]{:T(128)} %constant.15.clone.1), dimensions={0}, to_apply=%region_5.6 | reduce | flops 22020096 | bytes 113246208 | tf_op jit(solution)/shard_map/reduce_sum | solution.py:93
  (293 shorter events, 356.7 us)
Async XLA Ops:
  7.2 179.4 %copy-start = (f32[4,2048]{1,0:T(4,128)S(1)}, f32[4,2048]{1,0:T(4,128)}, u32[]{:S(2)}) copy-start(f32[4,2048]{1,0:T(4,128)} %param.10) | copy-start | bytes 98308
  7.2 159.9 %copy-start.20 = (f32[2048]{0:T(1024)S(1)}, f32[2048]{0:T(1024)}, u32[]{:S(2)}) copy-start(f32[2048]{0:T(1024)} %param.11) | copy-start | bytes 24580
  7.2 159.9 %copy-start.30 = (f32[2048]{0:T(1024)S(1)}, f32[2048]{0:T(1024)}, u32[]{:S(2)}) copy-start(f32[2048]{0:T(1024)} %param.12) | copy-start | bytes 24580
  7.2 159.9 %all-gather.4.cloned.1.call-start = ((), (), s32[]{:S(2)}) async-start(), calls=%async_computation.1 | async-start | bytes 31457280 | tf_op jit(solution)/shard_map/all_gather | solution.py:27
  8.0 1138.5 %reduce-scatter.2.cloned.1.call-start = ((), (), s32[]{:S(2)}) async-start(), calls=%async_computation.2 | async-start | bytes 62914560 | tf_op jit(solution)/shard_map/reduce_scatter | solution.py:71
  8.8 177.8 %copy-start.34 = (pred[512]{0:T(512)(128)(4,1)}, pred[512]{0:T(512)(128)(4,1)S(1)}, u32[]{:S(2)}) copy-start(pred[512]{0:T(512)(128)(4,1)S(1)} %pad_add_fusion.2) | copy-start | bytes 1540
  9.2 177.4 %copy-start.22 = (f32[512]{0:T(512)}, f32[512]{0:T(512)S(1)}, u32[]{:S(2)}) copy-start(f32[512]{0:T(512)S(1)} %broadcast_multiply_fusion.2) | copy-start | bytes 6148
  9.9 176.7 %copy-start.26 = (f32[512]{0:T(512)}, f32[512]{0:T(512)S(1)}, u32[]{:S(2)}) copy-start(f32[512]{0:T(512)S(1)} %add_rsqrt_fusion) | copy-start | bytes 6148
  355.5 7.0 copy-start.19
  379.5 9.8 copy-start.15
  436.1 6.9 copy-start.2
  436.1 6.9 copy-start.3
  436.1 8.0 copy-start.13
  436.1 8.0 copy-start.21
  436.1 8.0 copy-start.23
  436.1 8.0 copy-start.27
  436.1 8.0 copy-start.31
  634.9 17.5 copy-start.18
  668.8 9.7 copy-start.16
  731.8 32.6 %copy-start.35 = (pred[512]{0:T(512)(128)(4,1)S(1)}, pred[512]{0:T(512)(128)(4,1)}, u32[]{:S(2)}) copy-start(pred[512]{0:T(512)(128)(4,1)} %copy-done.34) | copy-start | bytes 1540
  764.4 10.8 copy-start.32
  799.9 2245.7 %all-gather.6.cloned.1.call-start = ((), (), s32[]{:S(2)}) async-start(), calls=%async_computation.3 | async-start | bytes 113246208 | tf_op jit(solution)/shard_map/all_gather | solution.py:92
  1147.2 180.6 %copy-start.25 = (s32[1,512]{1,0:T(1,128)S(1)}, s32[1,512]{1,0:T(1,128)}, u32[]{:S(2)}) copy-start(s32[1,512]{1,0:T(1,128)} %param.9) | copy-start | bytes 6148
  3045.5 36.2 %copy-start.1 = (f32[4,2048]{1,0:T(4,128)S(1)}, f32[4,2048]{1,0:T(4,128)}, u32[]{:S(2)}) copy-start(f32[4,2048]{1,0:T(4,128)} %param.10) | copy-start | bytes 98308
  (15 other events, 50.9 us)
Sparse Core Ops, SparseCore 0:
  9.6 157.4 all-gather.3
  800.0 346.4 reduce-scatter.1
  1148.0 1897.4 all-gather.5
